TPU v7x, 256 devices: a whole 4x4x8 slice. The times are simulated.
256 devices in a mesh: rows: 16 (over z_lo, x), tm: 16 (over y, z_hi, core).
Axes of the slice: x: 4, y: 4, z: 8 (z_hi: 2, z_lo: 4; z = z_hi * 4 + z_lo), core: 2. Of those that a mesh axis runs over, the one named last changes fastest.
Arguments:
- raw_signal: float32 [1024, 128, 128], P('tm', 'rows'), may hold values from -6 to 6
- fir_taps: float32 [61], replicated, may hold values from -0.75 to 0.75
- white_coef: float32 [25, 128, 128], P(None, 'rows'), may hold values from -1.25 to 1.25
- templates: bfloat16 [64, 61, 25], replicated, may hold values from -0.15625 to 0.15625
Outputs:
- whitened: bfloat16 [1024, 128, 128], P('tm', 'rows')
- best_score: float32 [1024, 128, 128], P('tm', 'rows')
All inputs are finite; a program needn't handle non-finite values.
Results may differ from a plain program's by a relative error of at most 0.0049.
Values may be sent and summed in bfloat16 or wider, within the bound.
No kernel may reach another device: no remote copies, remote signals or barrier semaphores. Data moves between devices by JAX's collectives and lax.ppermute only.
A program may use at most 64 MiB of HBM per device.

v0:
```python
import jax
import jax.numpy as jnp
from jax import lax
from jax.experimental import pallas as pl
from jax.experimental.pallas import tpu as pltpu
from jax.sharding import PartitionSpec as P


F32 = jnp.float32
BF16 = jnp.bfloat16
SHIFT = 4


def vmem():
    return pl.BlockSpec(memory_space=pltpu.VMEM)


def params(mib):
    return pltpu.CompilerParams(vmem_limit_bytes=mib * 1024 * 1024)


def swap_pairs(array, axis, first):
    size = lax.axis_size(axis)
    pairs = []
    for low in range(first, size - 1, 2):
        pairs += [(low, low + 1), (low + 1, low)]
    return lax.ppermute(array, axis, pairs)


def is_upper():
    return lax.rem(lax.axis_index("rows"), 2) == 0


def open_kernel(raw_ref, far_ref, keep_ref):
    skip = raw_ref.shape[0] - far_ref.shape[0]
    even = lax.rem(lax.axis_index("tm"), 2) == 0
    start = pl.multiple_of(jnp.where(even, 0, skip), 16)
    far_ref[...] = raw_ref[pl.ds(start, far_ref.shape[0]), :].astype(BF16)
    keep_ref[...] = raw_ref[...]


def opening(raw, rows, taps):
    return pl.pallas_call(
        open_kernel,
        out_shape=(
            jax.ShapeDtypeStruct(((taps - 1) * rows, raw.shape[1]), BF16),
            jax.ShapeDtypeStruct(raw.shape, F32),
        ),
        in_specs=[vmem()],
        out_specs=(vmem(), vmem()),
        compiler_params=params(4),
        cost_estimate=pl.CostEstimate(flops=10**5, bytes_accessed=10**6, transcendentals=0),
        name="opening",
    )(raw)


def prep_kernel(
    line_ref, tmpl_ref, coef_in_ref, band_ref, sum_ref, even_ref, odd_ref, coef_ref, wide, mixed
):
    _, count, length = tmpl_ref.shape
    own_rows = coef_ref.shape[0]
    upper = is_upper()
    for a in range(5):
        source = jnp.where(upper, a, 4 - a) * (5 * own_rows)
        for r in range(own_rows):
            line = pl.ds(source + jnp.where(upper, r, own_rows - 1 - r), 5, stride=own_rows)
            coef_ref[r, 5 * a : 5 * a + 5, :] = coef_in_ref[line, :]
    rows = band_ref.shape[0]
    line = jnp.broadcast_to(line_ref[...], (rows, 256))
    band = pltpu.roll(line, 0, 1, stride=1, stride_axis=0)
    high = band.astype(BF16)
    low = (band - high.astype(F32)).astype(BF16)
    band_ref[:, 0:256] = high
    band_ref[:, 256:512] = low
    band_ref[:, 512:768] = high

    wide[...] = jnp.zeros_like(wide)
    for a in range(5):
        source = jnp.where(upper, a, 4 - a) * 5
        for b in range(5):
            wide[5 * a + b, :, 0:length] = tmpl_ref[source + b].astype(F32)

    def even_spot(k):
        return wide[10 * (k // 5) + k % 5]

    def odd_spot(k):
        return wide[10 * (k // 5) + 5 + k % 5]

    def both_spots(k):
        return even_spot(k) + odd_spot(k) if k < 10 else even_spot(k)

    slot = 0
    for out_ref, piece, size in ((sum_ref, both_spots, 15), (even_ref, even_spot, 15), (odd_ref, odd_spot, 10)):
        for p in range(0, size, 2):
            pair = piece(p)
            if p + 1 < size:
                pair = pair + pltpu.roll(piece(p + 1), 64, 1)
            for b in range(SHIFT):
                moved = pltpu.roll(pair, b, 1) if b else pair
                mixed[slot, pl.ds(b, count, stride=SHIFT), :] = moved
            out_ref[:, 64 * p : 64 * p + 128] = mixed[slot].astype(BF16)
            slot += 1


def prep(fir_taps, templates, coef, span, rows):
    count, _, spots = templates.shape
    taps = fir_taps.shape[0]
    line = jnp.pad(fir_taps[::-1], (span - taps + 1, 255 - span))[None]
    by_spot = jnp.transpose(templates, (2, 0, 1))
    return pl.pallas_call(
        prep_kernel,
        out_shape=(
            jax.ShapeDtypeStruct((2 * span, 768), BF16),
            jax.ShapeDtypeStruct((count * SHIFT, 16 * 64), BF16),
            jax.ShapeDtypeStruct((count * SHIFT, 16 * 64), BF16),
            jax.ShapeDtypeStruct((count * SHIFT, 10 * 64), BF16),
            jax.ShapeDtypeStruct((rows, 32, coef.shape[1]), F32),
        ),
        in_specs=[vmem()] * 3,
        out_specs=(vmem(),) * 5,
        scratch_shapes=[
            pltpu.VMEM((spots, count, 128), F32),
            pltpu.VMEM((21, count * SHIFT, 128), F32),
        ],
        compiler_params=params(8),
        cost_estimate=pl.CostEstimate(flops=10**7, bytes_accessed=2 * 10**6, transcendentals=0),
        name="prep",
    )(line, by_spot, coef)


def fir_kernel(band_ref, raw_ref, near_ref, far_ref, coef_ref, filt_ref, first_ref, second_ref, widened, block):
    rows, double, cols = filt_ref.shape
    span = double // 2
    half = rows // 2
    even = lax.rem(lax.axis_index("tm"), 2) == 0
    short = far_ref.shape[0]
    skip = widened.shape[0] - short
    widened[0:skip, :] = jnp.zeros((skip, cols), F32)
    widened[short:, :] = jnp.zeros((skip, cols), F32)
    widened[pl.ds(pl.multiple_of(jnp.where(even, skip, 0), 16), short), :] = far_ref[...].astype(F32)
    columns = []
    upper = is_upper()
    for r in range(rows):
        line = pl.ds(jnp.where(upper, r, rows - 1 - r), span, stride=rows)
        near = near_ref[line, :]
        far = widened[line, :]
        own = raw_ref[line, :]
        before = jnp.where(even, far, near)
        after = jnp.where(even, near, far)
        line = jnp.concatenate([before, own, after, jnp.zeros_like(own)], axis=0)
        high = line.astype(BF16)
        low = (line - high.astype(F32)).astype(BF16)
        columns.append(jnp.concatenate([high, high, low], axis=0))
    for r in range(0, rows, 2):
        pair = jnp.concatenate(columns[r : r + 2], axis=1)
        out = jnp.dot(band_ref[...], pair, preferred_element_type=F32).astype(BF16)
        filt_ref[r] = out[:, :cols]
        filt_ref[r + 1] = out[:, cols:]
    base = half * double
    for side, order, edge in (
        (first_ref, range(rows - 1, rows - half - 1, -1), (rows - 1, rows - 2)),
        (second_ref, range(half - 1, -1, -1), (1, 0)),
    ):
        for k, r in enumerate(order):
            side[double * k : double * (k + 1), :] = filt_ref[r]
        for k, r in enumerate(edge):
            block[...] = jnp.zeros_like(block)
            for a in range(5):
                block[5 * a : 5 * a + 5, :] = coef_ref[r, 20 - 5 * a : 25 - 5 * a, :]
            side[base + 32 * k : base + 32 * k + 32, :] = block[...].astype(BF16)


def fir(band, raw, near, far, coef, rows):
    span = raw.shape[0] // rows
    cols = raw.shape[1]
    message = jax.ShapeDtypeStruct((rows // 2 * 2 * span + 64, cols), BF16)
    return pl.pallas_call(
        fir_kernel,
        out_shape=(jax.ShapeDtypeStruct((rows, 2 * span, cols), BF16), message, message),
        in_specs=[vmem()] * 5,
        out_specs=(vmem(),) * 3,
        scratch_shapes=[pltpu.VMEM(raw.shape, F32), pltpu.VMEM(coef.shape[1:], F32)],
        compiler_params=params(8),
        cost_estimate=pl.CostEstimate(flops=2 * 10**8, bytes_accessed=2 * 10**6, transcendentals=0),
        name="fir",
    )(band, raw, near, far, coef)


def shifter(shape):
    cols = shape[1]
    lane = lax.broadcasted_iota(jnp.int32, shape, 1)

    def shifted(x, b):
        if b == 2:
            return x
        out = pltpu.roll(x, (2 - b) % cols, 1)
        valid = lane >= 2 - b if b < 2 else lane < cols + 2 - b
        return jnp.where(valid, out, 0.0)

    return shifted


def closer(shape):
    span = shape[0] // 2
    last = lax.axis_index("tm") == lax.axis_size("tm") - 1
    time = lax.broadcasted_iota(jnp.int32, shape, 0)
    keep = jnp.logical_not(jnp.logical_and(last, time >= span))

    def closed(x):
        return jnp.where(keep, x, 0.0).astype(BF16).astype(F32)

    return closed


def build_slab(slab, x, shifted):
    double = x.shape[0]
    for b in range(5):
        moved = shifted(x, b)
        later = pltpu.roll(moved, double - SHIFT, 0)
        for f in range(4):
            piece = (later if f % 2 else moved)[8 * (f // 2) : 8 * (f // 2) + double - 16]
            slab[f, b] = piece.astype(BF16)


def inner_kernel(filt_ref, coef_ref, moved_ref, part_ref, white_ref, slab_ref):
    rows, double, cols = filt_ref.shape
    shifted = shifter((double, cols))
    closed = closer((double, cols))

    def spread(r, _):
        x = filt_ref[r].astype(F32)
        for b in range(5):
            moved_ref[b, r] = shifted(x, b)
        return 0

    lax.fori_loop(0, rows, spread, 0)

    def sums(r):
        total = jnp.zeros((double, cols), F32)
        for a in range(5):
            if 0 <= r + a - 2 < rows:
                for b in range(5):
                    s = 5 * a + b
                    total = total + coef_ref[r, s : s + 1, :] * moved_ref[b, r + a - 2]
        return total

    for k, r in enumerate((0, 1, rows - 2, rows - 1)):
        part_ref[k] = sums(r)
    for r in range(2, rows - 2):
        white_ref[r - 2] = closed(sums(r))
    build_slab(slab_ref.at[0], white_ref[1], shifted)
    build_slab(slab_ref.at[1], white_ref[3], shifted)
    build_slab(slab_ref.at[2], white_ref[0] - white_ref[1], shifted)
    build_slab(slab_ref.at[3], white_ref[2] - white_ref[3], shifted)
    build_slab(slab_ref.at[4], white_ref[2] - white_ref[1], shifted)


def inner(filt, coef):
    rows, double, cols = filt.shape
    return pl.pallas_call(
        inner_kernel,
        out_shape=(
            jax.ShapeDtypeStruct((5, rows, double, cols), F32),
            jax.ShapeDtypeStruct((4, double, cols), F32),
            jax.ShapeDtypeStruct((rows - 4, double, cols), F32),
            jax.ShapeDtypeStruct((5, 4, 5, double - 16, cols), BF16),
        ),
        in_specs=[vmem()] * 2,
        out_specs=(vmem(),) * 4,
        compiler_params=params(12),
        cost_estimate=pl.CostEstimate(flops=10**9, bytes_accessed=10**7, transcendentals=0),
        name="inner",
    )(filt, coef)


def spread_halo(side, halo, edge, shifted):
    half, double = halo.shape[1:3]

    def spread(k, _):
        x = side[pl.ds(pl.multiple_of(k * double, double), double), :].astype(F32)
        for b in range(5):
            halo[b, k] = shifted(x, b)
        return 0

    lax.fori_loop(0, half, spread, 0)
    base = half * double
    for k in range(2):
        edge[k] = side[base + 32 * k : base + 32 * k + 32, :].astype(F32)


def gather(total, weights, lines):
    for s, piece in lines:
        total = total + weights[s : s + 1, :] * piece
    return total


def score_block(lhs, plain, level, step, f, start):
    def product(lhs_ref, source, depth):
        cols = source[0].shape[-1]
        blank = [jnp.zeros((64, cols), BF16)] * (depth % 2)
        columns = [
            jnp.concatenate(
                [source[m + j][f, b, pl.ds(start, 64), :] for j in range(depth) for b in range(5)] + blank, axis=0
            )
            for m in range(2)
        ]
        found = jnp.dot(lhs_ref[...], jnp.concatenate(columns, axis=1), preferred_element_type=F32)
        return found.reshape(found.shape[0] // 8, 8, 2 * cols)

    def top(found):
        high = jnp.max(found, axis=0)
        return jnp.maximum(high, pltpu.roll(high, 4, 0))

    sum_ref, even_ref, odd_ref = lhs
    shared = product(sum_ref, plain, 3)
    return top(product(even_ref, level, 3) + shared), top(product(odd_ref, step, 2) + shared)


def after_kernel(
    side_ref,
    moved_ref,
    part_ref,
    mid_ref,
    mid_slab_ref,
    coef_ref,
    sum_ref,
    even_ref,
    odd_ref,
    white_ref,
    half_ref,
    slab_ref,
    halo,
    edge,
    white,
):
    rows, double, cols = moved_ref.shape[1:]
    half = rows // 2
    shifted = shifter((double, cols))
    closed = closer((double, cols))
    spread_halo(side_ref, halo, edge, shifted)

    def lines(w, offsets):
        for a in offsets:
            row = w + a - half
            for b in range(5):
                yield 5 * a + b, moved_ref[b, row] if row < rows else halo[b, row - rows]

    zero = jnp.zeros((double, cols), F32)
    white[0] = closed(gather(part_ref[2], coef_ref.at[rows - 2], lines(rows, (4,))))
    white[1] = closed(gather(part_ref[3], coef_ref.at[rows - 1], lines(rows + 1, (3, 4))))
    white[2] = closed(gather(zero, edge.at[0], lines(rows + 2, range(5))))
    white[3] = closed(gather(zero, edge.at[1], lines(rows + 3, range(5))))
    white_ref[0] = white[0, 0 : double // 2]
    white_ref[1] = white[1, 0 : double // 2]
    build_slab(slab_ref.at[0], white[1], shifted)
    build_slab(slab_ref.at[1], white[3], shifted)
    build_slab(slab_ref.at[2], white[0] - white[1], shifted)
    build_slab(slab_ref.at[3], white[2] - white[3], shifted)
    build_slab(slab_ref.at[4], white[0] - mid_ref[rows - 5], shifted)
    build_slab(slab_ref.at[5], white[2] - white[1], shifted)

    low = [slab_ref.at[k] for k in range(6)]
    mids = [mid_slab_ref.at[k] for k in range(5)]
    plain, level, step = mids[0:2] + low[0:2], mids[2:4] + low[2:4], mids[4:5] + low[4:6]

    def score(q, _):
        start = pl.multiple_of(q * 16, 16)
        for f in range(4):
            found = score_block((sum_ref, even_ref, odd_ref), plain, level, step, f, start)
            for r in range(half):
                first_row = (q * 4 + f) * SHIFT * half + r
                piece = found[r % 2][0:SHIFT, cols * (r // 2) : cols * (r // 2 + 1)]
                half_ref[pl.ds(first_row, SHIFT, stride=half), :] = piece
        return 0

    lax.fori_loop(0, double // 2 // (4 * SHIFT), score, 0, unroll=True)


def after(side, inside, coef, bands):
    moved, part, mid, mid_slabs = inside
    rows, double, cols = moved.shape[1:]
    return pl.pallas_call(
        after_kernel,
        out_shape=(
            jax.ShapeDtypeStruct((2, double // 2, cols), F32),
            jax.ShapeDtypeStruct((double // 2 * rows // 2, cols), F32),
        ),
        in_specs=[vmem()] * 9,
        out_specs=(vmem(),) * 2,
        scratch_shapes=[
            pltpu.VMEM((6, 4, 5, double - 16, cols), BF16),
            pltpu.VMEM((5, rows // 2, double, cols), F32),
            pltpu.VMEM((2, 32, cols), F32),
            pltpu.VMEM((4, double, cols), F32),
        ],
        compiler_params=params(16),
        cost_estimate=pl.CostEstimate(flops=6 * 10**9, bytes_accessed=10**7, transcendentals=0),
        name="after",
    )(side, moved, part, mid, mid_slabs, coef, *bands)


def match_kernel(
    side_ref,
    moved_ref,
    part_ref,
    mid_ref,
    mid_slab_ref,
    low_ref,
    half_ref,
    coef_ref,
    sum_ref,
    even_ref,
    odd_ref,
    white_hbm,
    best_hbm,
    halo,
    edge,
    white,
    slabs,
    natural,
    rounded,
    best,
    sems,
):
    rows, double, cols = moved_ref.shape[1:]
    span = double // 2
    half = rows // 2
    shifted = shifter((double, cols))
    closed = closer((double, cols))
    upper = is_upper()

    def actual(r):
        return jnp.where(upper, r, rows - 1 - r)

    spread_halo(side_ref, halo, edge, shifted)

    def lines(w, offsets):
        for a in offsets:
            row = w + a
            for b in range(5):
                yield 5 * a + b, halo[b, row] if row < half else moved_ref[b, row - half]

    zero = jnp.zeros((double, cols), F32)
    white[0] = closed(gather(zero, edge.at[0], lines(0, range(5))))
    white[1] = closed(gather(zero, edge.at[1], lines(1, range(5))))
    white[2] = closed(gather(part_ref[0], coef_ref.at[0], lines(2, (0, 1))))
    white[3] = closed(gather(part_ref[1], coef_ref.at[1], lines(3, (0,))))
    for r in range(rows):
        if r < 2:
            line = white[r + 2, 0:span]
        elif r < rows - 2:
            line = mid_ref[r - 2, 0:span]
        else:
            line = low_ref[r - rows + 2]
        natural[pl.ds(actual(r), span, stride=rows), :] = line
    rounded[...] = natural[...].astype(BF16)
    white_copy = pltpu.make_async_copy(rounded, white_hbm, sems.at[span // (4 * SHIFT)])
    white_copy.start()

    build_slab(slabs.at[0], white[1], shifted)
    build_slab(slabs.at[1], white[3], shifted)
    build_slab(slabs.at[2], white[0] - white[1], shifted)
    build_slab(slabs.at[3], white[2] - white[3], shifted)
    build_slab(slabs.at[4], white[2] - white[1], shifted)
    build_slab(slabs.at[5], mid_ref[0] - white[3], shifted)
    for r in range(half):
        best[pl.ds(actual(half + r), span, stride=rows), :] = half_ref[pl.ds(r, span, stride=half), :]
    high = [slabs.at[k] for k in range(6)]
    mids = [mid_slab_ref.at[k] for k in range(5)]
    plain, level, step = high[0:2] + mids[0:2], high[2:4] + mids[2:4], high[4:6] + mids[4:5]

    chunk = 4 * SHIFT * rows

    def sent(q):
        part = pl.ds(pl.multiple_of(q * chunk, chunk), chunk)
        return pltpu.make_async_copy(best.at[part, :], best_hbm.at[part, :], sems.at[q])

    def score(q, _):
        start = pl.multiple_of(q * 16, 16)
        for f in range(4):
            found = score_block((sum_ref, even_ref, odd_ref), plain, level, step, f, start)
            for r in range(half):
                first_row = q * chunk + SHIFT * rows * f + actual(r)
                piece = found[r % 2][0:SHIFT, cols * (r // 2) : cols * (r // 2 + 1)]
                best[pl.ds(first_row, SHIFT, stride=rows), :] = piece
        sent(q).start()
        return 0

    parts = span // (4 * SHIFT)
    lax.fori_loop(0, parts, score, 0, unroll=True)
    for q in range(parts):
        sent(q).wait()
    white_copy.wait()


def match(inside, lower, second, coef, bands):
    moved, part, mid, mid_slabs = inside
    rows, double, cols = moved.shape[1:]
    span = double // 2
    return pl.pallas_call(
        match_kernel,
        out_shape=(
            jax.ShapeDtypeStruct((span * rows, cols), BF16),
            jax.ShapeDtypeStruct((span * rows, cols), F32),
        ),
        in_specs=[vmem()] * 11,
        out_specs=(pl.BlockSpec(memory_space=pltpu.HBM),) * 2,
        scratch_shapes=[
            pltpu.VMEM((5, rows // 2, double, cols), F32),
            pltpu.VMEM((2, 32, cols), F32),
            pltpu.VMEM((4, double, cols), F32),
            pltpu.VMEM((6, 4, 5, double - 16, cols), BF16),
            pltpu.VMEM((span * rows, cols), F32),
            pltpu.VMEM((span * rows, cols), BF16),
            pltpu.VMEM((span * rows, cols), F32),
            pltpu.SemaphoreType.DMA((span // (4 * SHIFT) + 1,)),
        ],
        compiler_params=params(16),
        cost_estimate=pl.CostEstimate(flops=6 * 10**9, bytes_accessed=10**7, transcendentals=0),
        name="match",
    )(second, moved, part, mid, mid_slabs, *lower, coef, *bands)


def shards(raw_signal, fir_taps, white_coef, templates):
    span, rows, cols = raw_signal.shape
    raw = raw_signal.reshape(span * rows, cols)
    coef = white_coef.reshape(-1, cols)
    far, raw = opening(raw, rows, fir_taps.shape[0])
    far = swap_pairs(far, "tm", 1)
    near = swap_pairs(raw, "tm", 0)
    band, *bands, coef = prep(fir_taps, templates, coef, span, rows)
    filt, first, second = fir(band, raw, near, far, coef, rows)
    first = swap_pairs(first, "rows", 0)
    second = swap_pairs(second, "rows", 1)
    inside = inner(filt, coef)
    lower = after(first, inside, coef, bands)
    whitened, best = match(inside, lower, second, coef, bands)
    return whitened.reshape(span, rows, cols), best.reshape(span, rows, cols)


def solution(mesh):
    return jax.shard_map(
        shards,
        mesh=mesh,
        in_specs=(P("tm", "rows", None), P(), P(None, "rows", None), P()),
        out_specs=(P("tm", "rows", None), P("tm", "rows", None)),
        check_vma=False,
    )
```

profile of v0, /device:TPU:14, one launch (start us, length us, event | category | flops | bytes accessed | tf_op | source)
XLA Modules:
  0.0 39.2 jit_solution(865615137943651287)
XLA Ops:
  0.6 0.0 copy-start.1
  0.6 0.9 %copy-done.1 = f32[64,8,128]{2,1,0:T(8,128)S(1)} copy-done((f32[64,8,128]{2,1,0:T(8,128)S(1)}, f32[64,8,128]{2,1,0:T(8,128)}, u32[]{:S(2)}) %copy-start.1) | copy-done | bytes 262168
  1.6 0.1 collective-permute-start
  1.7 9.1 %collective-permute-start.1 = (bf16[480,128]{1,0:T(8,128)(2,1)S(1)}, bf16[480,128]{1,0:T(8,128)(2,1)S(1)}, u32[]{:S(2)}, u32[]{:S(2)}) collective-permute-start(bf16[480,128]{1,0:T(8,128)(2,1)S(1)} %get-tuple-element.22), channel_id=1, source_target_pairs={{1,2},{2,1},{3,4},{4,3},{5,6},{6,5},{7,8},{8,7},{9,10},{10,9},{11,... | collective-permute-start | bytes 368648 | tf_op jit(solution)/shard_map/ppermute | solution.py:27
  10.8 0.7 %rev.3 = f32[61]{0:T(128)S(1)} reverse(f32[61]{0:T(128)} %param.5), dimensions={0} | reverse | bytes 488 | tf_op jit(solution)/shard_map/rev | solution.py:108
  11.5 0.1 pad.4
  11.6 0.0 copy-start
  11.6 1.0 %copy-done = bf16[64,61,25]{1,0,2:T(8,128)(2,1)S(1)} copy-done((bf16[64,61,25]{1,0,2:T(8,128)(2,1)S(1)}, bf16[64,61,25]{1,0,2:T(8,128)(2,1)}, u32[]{:S(2)}) %copy-start) | copy-done | bytes 195224
  12.6 0.0 copy-start.2
  12.6 0.9 %copy-done.2 = f32[25,8,128]{2,1,0:T(8,128)S(1)} copy-done((f32[25,8,128]{2,1,0:T(8,128)S(1)}, f32[25,8,128]{2,1,0:T(8,128)}, u32[]{:S(2)}) %copy-start.2) | copy-done | bytes 102424
  13.5 2.1 %prep.1 = (bf16[128,768]{1,0:T(8,128)(2,1)S(1)}, bf16[256,1024]{1,0:T(8,128)(2,1)S(1)}, bf16[256,1024]{1,0:T(8,128)(2,1)S(1)}, bf16[256,640]{1,0:T(8,128)(2,1)S(1)}, f32[8,32,128]{2,1,0:T(8,128)S(1)}) custom-call(f32[1,256]{1,0:T(1,128)S(1)} %bitcast.9, bf16[25,64,61]{2,1,0:T(8,128)(2,1)S(1)} %bitcast.6, f32[200,128]{1,0:T(8,128)S(1)} %bitcast.8), custom_call_target="tpu_custom_call" | custom-call | flops 10000000 | bytes 2000000 | tf_op jit(solution)/shard_map/prep/pallas_call | solution.py:110
  15.6 0.0 collective-permute-done.1.far_ref
  15.6 0.0 collective-permute-done.near_ref
  15.6 0.6 %fir.1 = (bf16[8,128,128]{2,1,0:T(8,128)(2,1)S(1)}, bf16[576,128]{1,0:T(8,128)(2,1)S(1)}, bf16[576,128]{1,0:T(8,128)(2,1)S(1)}) custom-call(bf16[128,768]{1,0:T(8,128)(2,1)S(1)} %get-tuple-element.20.band_ref, f32[512,128]{1,0:T(8,128)S(1)} %get-tuple-element.21.raw_ref, f32[512,128]{1,0:T(8,128)S(1)} %collective-permute-done.near_ref, ...), custom_call_target="tpu_custom_call" | custom-call | flops 200000000 | bytes 2000000 | tf_op jit(solution)/shard_map/fir/pallas_call | solution.py:177
  16.2 0.9 %collective-permute-start.3 = (bf16[576,128]{1,0:T(8,128)(2,1)S(1)}, bf16[576,128]{1,0:T(8,128)(2,1)S(1)}, u32[]{:S(2)}, u32[]{:S(2)}) collective-permute-start(bf16[576,128]{1,0:T(8,128)(2,1)S(1)} %get-tuple-element.30), channel_id=1, source_target_pairs={{0,16},{16,0},{32,48},{48,32},{64,80},{80,64},{96,112},{112,96},{1... | collective-permute-start | bytes 442376 | tf_op jit(solution)/shard_map/ppermute | solution.py:27
  17.1 5.2 %collective-permute-start.2 = (bf16[576,128]{1,0:T(8,128)(2,1)S(1)}, bf16[576,128]{1,0:T(8,128)(2,1)S(1)}, u32[]{:S(2)}, u32[]{:S(2)}) collective-permute-start(bf16[576,128]{1,0:T(8,128)(2,1)S(1)} %get-tuple-element.24), channel_id=1, source_target_pairs={{16,32},{32,16},{48,64},{64,48},{80,96},{96,80},{112,128},{128,112... | collective-permute-start | bytes 442376 | tf_op jit(solution)/shard_map/ppermute | solution.py:27
  22.4 1.9 %inner.1 = (f32[5,8,128,128]{3,2,1,0:T(8,128)S(1)}, f32[4,128,128]{2,1,0:T(8,128)S(1)}, f32[4,128,128]{2,1,0:T(8,128)S(1)}, bf16[5,4,5,112,128]{4,3,2,1,0:T(8,128)(2,1)S(1)}) custom-call(bf16[8,128,128]{2,1,0:T(8,128)(2,1)S(1)} %get-tuple-element.25.filt_ref, f32[8,32,128]{2,1,0:T(8,128)S(1)} %get-tuple-element.23.coef_ref), custom_call_target="tpu_custom_call" | custom-call | flops 1000000000 | bytes 10000000 | tf_op jit(solution)/shard_map/inner/pallas_call | solution.py:260
  24.3 0.0 collective-permute-done.3.side_ref
  24.3 6.9 %after.1 = (f32[2,64,128]{2,1,0:T(8,128)S(1)}, f32[256,128]{1,0:T(8,128)S(1)}) custom-call(bf16[576,128]{1,0:T(8,128)(2,1)S(1)} %collective-permute-done.3.side_ref, f32[5,8,128,128]{3,2,1,0:T(8,128)S(1)} %get-tuple-element.26.moved_ref, f32[4,128,128]{2,1,0:T(8,128)S(1)} %get-tuple-element.27.part_ref, f32[4,128,128]{2,1,0:T(8,128)S(1)} %get-tuple-element.28.mid_ref, ...), custom_call_target="tpu_custom_call" | custom-call | flops 6000000000 | bytes 10000000 | tf_op jit(solution)/shard_map/after/pallas_call | solution.py:382
  31.2 0.0 collective-permute-done.2.side_ref
  31.2 7.9 %match.1 = (bf16[512,128]{1,0:T(8,128)(2,1)}, f32[512,128]{1,0:T(8,128)}) custom-call(bf16[576,128]{1,0:T(8,128)(2,1)S(1)} %collective-permute-done.2.side_ref, f32[5,8,128,128]{3,2,1,0:T(8,128)S(1)} %get-tuple-element.26.moved_ref, f32[4,128,128]{2,1,0:T(8,128)S(1)} %get-tuple-element.27.part_ref, f32[4,128,128]{2,1,0:T(8,128)S(1)} %get-tuple-element.28.mid_ref, ...), custom_call_target="tpu_custom_call" | custom-call | flops 6000000000 | bytes 10000000 | tf_op jit(solution)/shard_map/match/pallas_call | solution.py:500
  (1 shorter events, 0.0 us)
Async XLA Ops:
  0.6 1.0 %copy-start.1 = (f32[64,8,128]{2,1,0:T(8,128)S(1)}, f32[64,8,128]{2,1,0:T(8,128)}, u32[]{:S(2)}) copy-start(f32[64,8,128]{2,1,0:T(8,128)} %param.4) | copy-start | bytes 786436
  1.6 14.0 %collective-permute-start = (f32[512,128]{1,0:T(8,128)S(1)}, f32[512,128]{1,0:T(8,128)S(1)}, u32[]{:S(2)}, u32[]{:S(2)}) collective-permute-start(f32[512,128]{1,0:T(8,128)S(1)} %get-tuple-element.21.raw_ref), channel_id=1, source_target_pairs={{0,1},{1,0},{2,3},{3,2},{4,5},{5,4},{6,7},{7,6},{8,9},{9,8},{10,11... | collective-permute-start | bytes 786440 | tf_op jit(solution)/shard_map/ppermute | solution.py:27
  1.7 13.9 %collective-permute-start.1 = (bf16[480,128]{1,0:T(8,128)(2,1)S(1)}, bf16[480,128]{1,0:T(8,128)(2,1)S(1)}, u32[]{:S(2)}, u32[]{:S(2)}) collective-permute-start(bf16[480,128]{1,0:T(8,128)(2,1)S(1)} %get-tuple-element.22), channel_id=1, source_target_pairs={{1,2},{2,1},{3,4},{4,3},{5,6},{6,5},{7,8},{8,7},{9,10},{10,9},{11,... | collective-permute-start | bytes 368648 | tf_op jit(solution)/shard_map/ppermute | solution.py:27
  11.6 1.0 %copy-start = (bf16[64,61,25]{1,0,2:T(8,128)(2,1)S(1)}, bf16[64,61,25]{1,0,2:T(8,128)(2,1)}, u32[]{:S(2)}) copy-start(bf16[64,61,25]{1,0,2:T(8,128)(2,1)} %param.7) | copy-start | bytes 585604
  12.6 0.9 %copy-start.2 = (f32[25,8,128]{2,1,0:T(8,128)S(1)}, f32[25,8,128]{2,1,0:T(8,128)}, u32[]{:S(2)}) copy-start(f32[25,8,128]{2,1,0:T(8,128)} %param.6) | copy-start | bytes 307204
  16.2 8.1 %collective-permute-start.3 = (bf16[576,128]{1,0:T(8,128)(2,1)S(1)}, bf16[576,128]{1,0:T(8,128)(2,1)S(1)}, u32[]{:S(2)}, u32[]{:S(2)}) collective-permute-start(bf16[576,128]{1,0:T(8,128)(2,1)S(1)} %get-tuple-element.30), channel_id=1, source_target_pairs={{0,16},{16,0},{32,48},{48,32},{64,80},{80,64},{96,112},{112,96},{1... | collective-permute-start | bytes 442376 | tf_op jit(solution)/shard_map/ppermute | solution.py:27
  17.1 14.0 %collective-permute-start.2 = (bf16[576,128]{1,0:T(8,128)(2,1)S(1)}, bf16[576,128]{1,0:T(8,128)(2,1)S(1)}, u32[]{:S(2)}, u32[]{:S(2)}) collective-permute-start(bf16[576,128]{1,0:T(8,128)(2,1)S(1)} %get-tuple-element.24), channel_id=1, source_target_pairs={{16,32},{32,16},{48,64},{64,48},{80,96},{96,80},{112,128},{128,112... | collective-permute-start | bytes 442376 | tf_op jit(solution)/shard_map/ppermute | solution.py:27
where the time goes:
time: 39.9 us; the launch traced here: 39.2 us
  Pallas kernels  19.3 us (48%)
  starting transfers between devices  15.3 us (38%)
  local copies, waits for them, and re-layouts  3.66 us (9%)
  between operations  0.89 us (2%)
    ppermute x4, starting transfers between devices, swap_pairs(): return lax.ppermute(array, axis, pairs)  15.3 us
    pallas_call x1, Pallas kernels, match(): pl.pallas_call(match_kernel, out_shape=(jax.ShapeDtypeStruct((span * rows...  7.89 us
    pallas_call x1, Pallas kernels, after(): pl.pallas_call(after_kernel, out_shape=(jax.ShapeDtypeStruct((2, double /...  6.86 us
    unnamed x6, local copies, waits for them, and re-layouts  2.84 us
    pallas_call x1, Pallas kernels, prep(): pl.pallas_call(prep_kernel, out_shape=(jax.ShapeDtypeStruct((2 * span, 76...  2.05 us
    pallas_call x1, Pallas kernels, inner(): pl.pallas_call(inner_kernel, out_shape=(jax.ShapeDtypeStruct((5, rows, do...  1.91 us
  transfers between devices with their start and end apart: 4, of which 0 were waited for; matrix products, arithmetic and copies ran while one was open for 2% of the time, Pallas kernels for 28%

commit v1 on v0

--- a/solution.py
+++ b/solution.py
@@ -282,7 +282,7 @@
             halo[b, k] = shifted(x, b)
         return 0
 
-    lax.fori_loop(0, half, spread, 0)
+    lax.fori_loop(0, half, spread, 0, unroll=True)
     base = half * double
     for k in range(2):
         edge[k] = side[base + 32 * k : base + 32 * k + 32, :].astype(F32)
@@ -373,7 +373,7 @@
                 half_ref[pl.ds(first_row, SHIFT, stride=half), :] = piece
         return 0
 
-    lax.fori_loop(0, double // 2 // (4 * SHIFT), score, 0, unroll=True)
+    lax.fori_loop(0, double // 2 // (8 * SHIFT), score, 0, unroll=True)
 
 
 def after(side, inside, coef, bands):
@@ -383,12 +383,12 @@
         after_kernel,
         out_shape=(
             jax.ShapeDtypeStruct((2, double // 2, cols), F32),
-            jax.ShapeDtypeStruct((double // 2 * rows // 2, cols), F32),
+            jax.ShapeDtypeStruct((double // 4 * rows // 2, cols), F32),
+            jax.ShapeDtypeStruct((6, 4, 5, double - 16, cols), BF16),
         ),
         in_specs=[vmem()] * 9,
-        out_specs=(vmem(),) * 2,
+        out_specs=(vmem(),) * 3,
         scratch_shapes=[
-            pltpu.VMEM((6, 4, 5, double - 16, cols), BF16),
             pltpu.VMEM((5, rows // 2, double, cols), F32),
             pltpu.VMEM((2, 32, cols), F32),
             pltpu.VMEM((4, double, cols), F32),
@@ -407,6 +407,7 @@
     mid_slab_ref,
     low_ref,
     half_ref,
+    low_slab_ref,
     coef_ref,
     sum_ref,
     even_ref,
@@ -432,7 +433,23 @@
     def actual(r):
         return jnp.where(upper, r, rows - 1 - r)
 
+    chunk = 4 * SHIFT * rows
+    parts = span // (4 * SHIFT)
+    lhs = (sum_ref, even_ref, odd_ref)
+    mids = [mid_slab_ref.at[k] for k in range(5)]
+    low = [low_slab_ref.at[k] for k in range(6)]
+
+    def place(found, q, f, offset):
+        for r in range(half):
+            first_row = q * chunk + SHIFT * rows * f + actual(offset + r)
+            piece = found[r % 2][0:SHIFT, cols * (r // 2) : cols * (r // 2 + 1)]
+            best[pl.ds(first_row, SHIFT, stride=rows), :] = piece
+
     spread_halo(side_ref, halo, edge, shifted)
+    for q in range(parts // 2, parts):
+        for f in range(4):
+            found = score_block(lhs, mids[0:2] + low[0:2], mids[2:4] + low[2:4], mids[4:5] + low[4:6], f, 16 * q)
+            place(found, q, f, half)
 
     def lines(w, offsets):
         for a in offsets:
@@ -464,12 +481,9 @@
     build_slab(slabs.at[4], white[2] - white[1], shifted)
     build_slab(slabs.at[5], mid_ref[0] - white[3], shifted)
     for r in range(half):
-        best[pl.ds(actual(half + r), span, stride=rows), :] = half_ref[pl.ds(r, span, stride=half), :]
+        best[pl.ds(actual(half + r), span // 2, stride=rows), :] = half_ref[pl.ds(r, span // 2, stride=half), :]
     high = [slabs.at[k] for k in range(6)]
-    mids = [mid_slab_ref.at[k] for k in range(5)]
     plain, level, step = high[0:2] + mids[0:2], high[2:4] + mids[2:4], high[4:6] + mids[4:5]
-
-    chunk = 4 * SHIFT * rows
 
     def sent(q):
         part = pl.ds(pl.multiple_of(q * chunk, chunk), chunk)
@@ -478,15 +492,10 @@
     def score(q, _):
         start = pl.multiple_of(q * 16, 16)
         for f in range(4):
-            found = score_block((sum_ref, even_ref, odd_ref), plain, level, step, f, start)
-            for r in range(half):
-                first_row = q * chunk + SHIFT * rows * f + actual(r)
-                piece = found[r % 2][0:SHIFT, cols * (r // 2) : cols * (r // 2 + 1)]
-                best[pl.ds(first_row, SHIFT, stride=rows), :] = piece
+            place(score_block(lhs, plain, level, step, f, start), q, f, 0)
         sent(q).start()
         return 0
 
-    parts = span // (4 * SHIFT)
     lax.fori_loop(0, parts, score, 0, unroll=True)
     for q in range(parts):
         sent(q).wait()
@@ -503,7 +512,7 @@
             jax.ShapeDtypeStruct((span * rows, cols), BF16),
             jax.ShapeDtypeStruct((span * rows, cols), F32),
         ),
-        in_specs=[vmem()] * 11,
+        in_specs=[vmem()] * 12,
         out_specs=(pl.BlockSpec(memory_space=pltpu.HBM),) * 2,
         scratch_shapes=[
             pltpu.VMEM((5, rows // 2, double, cols), F32),

time: 39.9 us -> 39.1 us (0.980)
  Pallas kernels: 19.3 us -> 18.5 us
    pallas_call x1, Pallas kernels: 6.86 us -> 3.58 us  [after(): pl.pallas_call(after_kernel, out_shape=(jax.ShapeDtypeStruct((2, double /...]
    pallas_call x1, Pallas kernels: 7.89 us -> 10.1 us  [match(): pl.pallas_call(match_kernel, out_shape=(jax.ShapeDtypeStruct((span * rows...]
  transfers between devices with their start and end apart: 4 -> 4, of which waited for: 0 -> 0; matrix products, arithmetic and copies ran while one was open for 2% -> 2% of each run, Pallas kernels for 28% -> 20%
where the time goes in v1:
time: 39.1 us; the launch traced here: 38.3 us
  Pallas kernels  18.5 us (47%)
  starting transfers between devices  15.3 us (39%)
  local copies, waits for them, and re-layouts  3.66 us (9%)
  between operations  0.89 us (2%)
    ppermute x4, starting transfers between devices, swap_pairs(): return lax.ppermute(array, axis, pairs)  15.3 us
    pallas_call x1, Pallas kernels, match(): pl.pallas_call(match_kernel, out_shape=(jax.ShapeDtypeStruct((span * rows...  10.1 us
    pallas_call x1, Pallas kernels, after(): pl.pallas_call(after_kernel, out_shape=(jax.ShapeDtypeStruct((2, double /...  3.58 us
    unnamed x6, local copies, waits for them, and re-layouts  2.84 us
    pallas_call x1, Pallas kernels, inner(): pl.pallas_call(inner_kernel, out_shape=(jax.ShapeDtypeStruct((5, rows, do...  2.09 us
    pallas_call x1, Pallas kernels, prep(): pl.pallas_call(prep_kernel, out_shape=(jax.ShapeDtypeStruct((2 * span, 76...  2.05 us
  transfers between devices with their start and end apart: 4, of which 0 were waited for; matrix products, arithmetic and copies ran while one was open for 2% of the time, Pallas kernels for 20%

profile of v1, /device:TPU:14, one launch (start us, length us, event | category | flops | bytes accessed | tf_op | source)
XLA Modules:
  0.0 38.3 jit_solution(4082984137093603122)
XLA Ops:
  0.6 0.0 copy-start.1
  0.6 0.9 %copy-done.1 = f32[64,8,128]{2,1,0:T(8,128)S(1)} copy-done((f32[64,8,128]{2,1,0:T(8,128)S(1)}, f32[64,8,128]{2,1,0:T(8,128)}, u32[]{:S(2)}) %copy-start.1) | copy-done | bytes 262168
  1.6 0.1 collective-permute-start
  1.7 9.1 %collective-permute-start.1 = (bf16[480,128]{1,0:T(8,128)(2,1)S(1)}, bf16[480,128]{1,0:T(8,128)(2,1)S(1)}, u32[]{:S(2)}, u32[]{:S(2)}) collective-permute-start(bf16[480,128]{1,0:T(8,128)(2,1)S(1)} %get-tuple-element.23), channel_id=1, source_target_pairs={{1,2},{2,1},{3,4},{4,3},{5,6},{6,5},{7,8},{8,7},{9,10},{10,9},{11,... | collective-permute-start | bytes 368648 | tf_op jit(solution)/shard_map/ppermute | solution.py:27
  10.8 0.7 %rev.3 = f32[61]{0:T(128)S(1)} reverse(f32[61]{0:T(128)} %param.5), dimensions={0} | reverse | bytes 488 | tf_op jit(solution)/shard_map/rev | solution.py:108
  11.5 0.1 pad.4
  11.6 0.0 copy-start
  11.6 1.0 %copy-done = bf16[64,61,25]{1,0,2:T(8,128)(2,1)S(1)} copy-done((bf16[64,61,25]{1,0,2:T(8,128)(2,1)S(1)}, bf16[64,61,25]{1,0,2:T(8,128)(2,1)}, u32[]{:S(2)}) %copy-start) | copy-done | bytes 195224
  12.6 0.0 copy-start.2
  12.6 0.9 %copy-done.2 = f32[25,8,128]{2,1,0:T(8,128)S(1)} copy-done((f32[25,8,128]{2,1,0:T(8,128)S(1)}, f32[25,8,128]{2,1,0:T(8,128)}, u32[]{:S(2)}) %copy-start.2) | copy-done | bytes 102424
  13.5 2.1 %prep.1 = (bf16[128,768]{1,0:T(8,128)(2,1)S(1)}, bf16[256,1024]{1,0:T(8,128)(2,1)S(1)}, bf16[256,1024]{1,0:T(8,128)(2,1)S(1)}, bf16[256,640]{1,0:T(8,128)(2,1)S(1)}, f32[8,32,128]{2,1,0:T(8,128)S(1)}) custom-call(f32[1,256]{1,0:T(1,128)S(1)} %bitcast.9, bf16[25,64,61]{2,1,0:T(8,128)(2,1)S(1)} %bitcast.6, f32[200,128]{1,0:T(8,128)S(1)} %bitcast.8), custom_call_target="tpu_custom_call" | custom-call | flops 10000000 | bytes 2000000 | tf_op jit(solution)/shard_map/prep/pallas_call | solution.py:110
  15.6 0.0 collective-permute-done.1.far_ref
  15.6 0.0 collective-permute-done.near_ref
  15.6 0.6 %fir.1 = (bf16[8,128,128]{2,1,0:T(8,128)(2,1)S(1)}, bf16[576,128]{1,0:T(8,128)(2,1)S(1)}, bf16[576,128]{1,0:T(8,128)(2,1)S(1)}) custom-call(bf16[128,768]{1,0:T(8,128)(2,1)S(1)} %get-tuple-element.21.band_ref, f32[512,128]{1,0:T(8,128)S(1)} %get-tuple-element.22.raw_ref, f32[512,128]{1,0:T(8,128)S(1)} %collective-permute-done.near_ref, ...), custom_call_target="tpu_custom_call" | custom-call | flops 200000000 | bytes 2000000 | tf_op jit(solution)/shard_map/fir/pallas_call | solution.py:177
  16.2 0.9 %collective-permute-start.3 = (bf16[576,128]{1,0:T(8,128)(2,1)S(1)}, bf16[576,128]{1,0:T(8,128)(2,1)S(1)}, u32[]{:S(2)}, u32[]{:S(2)}) collective-permute-start(bf16[576,128]{1,0:T(8,128)(2,1)S(1)} %get-tuple-element.31), channel_id=1, source_target_pairs={{0,16},{16,0},{32,48},{48,32},{64,80},{80,64},{96,112},{112,96},{1... | collective-permute-start | bytes 442376 | tf_op jit(solution)/shard_map/ppermute | solution.py:27
  17.1 5.2 %collective-permute-start.2 = (bf16[576,128]{1,0:T(8,128)(2,1)S(1)}, bf16[576,128]{1,0:T(8,128)(2,1)S(1)}, u32[]{:S(2)}, u32[]{:S(2)}) collective-permute-start(bf16[576,128]{1,0:T(8,128)(2,1)S(1)} %get-tuple-element.25), channel_id=1, source_target_pairs={{16,32},{32,16},{48,64},{64,48},{80,96},{96,80},{112,128},{128,112... | collective-permute-start | bytes 442376 | tf_op jit(solution)/shard_map/ppermute | solution.py:27
  22.4 2.1 %inner.1 = (f32[5,8,128,128]{3,2,1,0:T(8,128)S(1)}, f32[4,128,128]{2,1,0:T(8,128)S(1)}, f32[4,128,128]{2,1,0:T(8,128)S(1)}, bf16[5,4,5,112,128]{4,3,2,1,0:T(8,128)(2,1)S(1)}) custom-call(bf16[8,128,128]{2,1,0:T(8,128)(2,1)S(1)} %get-tuple-element.26.filt_ref, f32[8,32,128]{2,1,0:T(8,128)S(1)} %get-tuple-element.24.coef_ref), custom_call_target="tpu_custom_call" | custom-call | flops 1000000000 | bytes 10000000 | tf_op jit(solution)/shard_map/inner/pallas_call | solution.py:260
  24.5 0.0 collective-permute-done.3.side_ref
  24.5 3.6 %after.1 = (f32[2,64,128]{2,1,0:T(8,128)S(1)}, f32[128,128]{1,0:T(8,128)S(1)}, bf16[6,4,5,112,128]{4,3,2,1,0:T(8,128)(2,1)S(1)}) custom-call(bf16[576,128]{1,0:T(8,128)(2,1)S(1)} %collective-permute-done.3.side_ref, f32[5,8,128,128]{3,2,1,0:T(8,128)S(1)} %get-tuple-element.27.moved_ref, f32[4,128,128]{2,1,0:T(8,128)S(1)} %get-tuple-element.28.part_ref, ...), custom_call_target="tpu_custom_call" | custom-call | flops 6000000000 | bytes 10000000 | tf_op jit(solution)/shard_map/after/pallas_call | solution.py:382
  28.1 0.0 collective-permute-done.2.side_ref
  28.1 10.1 %match.1 = (bf16[512,128]{1,0:T(8,128)(2,1)}, f32[512,128]{1,0:T(8,128)}) custom-call(bf16[576,128]{1,0:T(8,128)(2,1)S(1)} %collective-permute-done.2.side_ref, f32[5,8,128,128]{3,2,1,0:T(8,128)S(1)} %get-tuple-element.27.moved_ref, f32[4,128,128]{2,1,0:T(8,128)S(1)} %get-tuple-element.28.part_ref, f32[4,128,128]{2,1,0:T(8,128)S(1)} %get-tuple-element.29.mid_ref, ...), custom_call_target="tpu_custom_call" | custom-call | flops 6000000000 | bytes 10000000 | tf_op jit(solution)/shard_map/match/pallas_call | solution.py:509
  (1 shorter events, 0.0 us)
Async XLA Ops:
  0.6 1.0 %copy-start.1 = (f32[64,8,128]{2,1,0:T(8,128)S(1)}, f32[64,8,128]{2,1,0:T(8,128)}, u32[]{:S(2)}) copy-start(f32[64,8,128]{2,1,0:T(8,128)} %param.4) | copy-start | bytes 786436
  1.6 14.0 %collective-permute-start = (f32[512,128]{1,0:T(8,128)S(1)}, f32[512,128]{1,0:T(8,128)S(1)}, u32[]{:S(2)}, u32[]{:S(2)}) collective-permute-start(f32[512,128]{1,0:T(8,128)S(1)} %get-tuple-element.22.raw_ref), channel_id=1, source_target_pairs={{0,1},{1,0},{2,3},{3,2},{4,5},{5,4},{6,7},{7,6},{8,9},{9,8},{10,11... | collective-permute-start | bytes 786440 | tf_op jit(solution)/shard_map/ppermute | solution.py:27
  1.7 13.9 %collective-permute-start.1 = (bf16[480,128]{1,0:T(8,128)(2,1)S(1)}, bf16[480,128]{1,0:T(8,128)(2,1)S(1)}, u32[]{:S(2)}, u32[]{:S(2)}) collective-permute-start(bf16[480,128]{1,0:T(8,128)(2,1)S(1)} %get-tuple-element.23), channel_id=1, source_target_pairs={{1,2},{2,1},{3,4},{4,3},{5,6},{6,5},{7,8},{8,7},{9,10},{10,9},{11,... | collective-permute-start | bytes 368648 | tf_op jit(solution)/shard_map/ppermute | solution.py:27
  11.6 1.0 %copy-start = (bf16[64,61,25]{1,0,2:T(8,128)(2,1)S(1)}, bf16[64,61,25]{1,0,2:T(8,128)(2,1)}, u32[]{:S(2)}) copy-start(bf16[64,61,25]{1,0,2:T(8,128)(2,1)} %param.7) | copy-start | bytes 585604
  12.6 0.9 %copy-start.2 = (f32[25,8,128]{2,1,0:T(8,128)S(1)}, f32[25,8,128]{2,1,0:T(8,128)}, u32[]{:S(2)}) copy-start(f32[25,8,128]{2,1,0:T(8,128)} %param.6) | copy-start | bytes 307204
  16.2 8.2 %collective-permute-start.3 = (bf16[576,128]{1,0:T(8,128)(2,1)S(1)}, bf16[576,128]{1,0:T(8,128)(2,1)S(1)}, u32[]{:S(2)}, u32[]{:S(2)}) collective-permute-start(bf16[576,128]{1,0:T(8,128)(2,1)S(1)} %get-tuple-element.31), channel_id=1, source_target_pairs={{0,16},{16,0},{32,48},{48,32},{64,80},{80,64},{96,112},{112,96},{1... | collective-permute-start | bytes 442376 | tf_op jit(solution)/shard_map/ppermute | solution.py:27
  17.1 10.9 %collective-permute-start.2 = (bf16[576,128]{1,0:T(8,128)(2,1)S(1)}, bf16[576,128]{1,0:T(8,128)(2,1)S(1)}, u32[]{:S(2)}, u32[]{:S(2)}) collective-permute-start(bf16[576,128]{1,0:T(8,128)(2,1)S(1)} %get-tuple-element.25), channel_id=1, source_target_pairs={{16,32},{32,16},{48,64},{64,48},{80,96},{96,80},{112,128},{128,112... | collective-permute-start | bytes 442376 | tf_op jit(solution)/shard_map/ppermute | solution.py:27
